TPU v7x, 256 devices: a whole 4x4x8 slice. The times are simulated.
256 devices in a mesh: seq: 32 (over x, z), head: 8 (over y, core).
Axes of the slice: x: 4, y: 4, z: 8, core: 2. Of those that a mesh axis runs over, the one named last changes fastest.
Arguments:
- tokens: bfloat16 [16384, 4096], P('seq'), may hold values from -6 to 6
- w_xz: bfloat16 [4096, 2, 4096], P('seq', None, 'head'), may hold values from -0.09375 to 0.09375
- w_bc: bfloat16 [4096, 256], P('seq'), may hold values from -0.09375 to 0.09375
- conv_x: float32 [4, 4096], P(None, 'head'), may hold values from -3 to 3
- conv_bc: float32 [4, 256], replicated, may hold values from -3 to 3
- tail_x: bfloat16 [3, 4096], P(None, 'head'), may hold values from -6 to 6
- tail_bc: bfloat16 [3, 256], replicated, may hold values from -6 to 6
- decay_code: int32 [16384, 64], P('seq', 'head'), may hold values from 0 to 196608, as said below
- skip_gain: float32 [64], P('head'), may hold values from 0.5 to 2
- state_in: float32 [64, 64, 128], P('head'), may hold values from -180 to 180
- norm_gain: float32 [4096], P('head'), may hold values from 0.1 to 1.9
- w_out: bfloat16 [4096, 4096], P('head', 'seq'), may hold values from -0.1875 to 0.1875
Outputs:
- mixed: bfloat16 [16384, 4096], P('seq', 'head')
Inputs may be any that keep to these rules, and one draw needn't show every extreme that they name: `decay_code`: the decay factor of a token and head is exp(-code / 262144).
All inputs are finite; a program needn't handle non-finite values.
Results may differ from a plain program's by a relative error of at most 0.0085.
Values may be sent and summed in bfloat16 or wider, within the bound.
A program may use at most 128 MiB of HBM per device.

v0:
```python
import jax
import jax.numpy as jnp
from jax import lax
from jax.sharding import PartitionSpec as P

Q = 256


def passed_along(value, axis, by):
    size = lax.axis_size(axis)
    pairs = [(i, i + by) for i in range(size) if 0 <= i + by < size]
    return lax.ppermute(value, axis, pairs)


def depthwise(pre, tail, kernel):
    whole = jnp.concatenate([tail, pre], axis=0).astype(jnp.float32)
    length = pre.shape[0]
    total = jnp.zeros((length, pre.shape[1]), jnp.float32)
    for offset in range(kernel.shape[0]):
        total = total + kernel[offset] * whole[offset : offset + length]
    return jax.nn.silu(total).astype(jnp.bfloat16)


def entering_state(decay, end_state, state_in):
    count = lax.axis_size("seq")
    me = lax.axis_index("seq")
    first = me == 0
    lanes = end_state.shape[2]

    def pack(a, s):
        return jnp.concatenate(
            [s, jnp.broadcast_to(a[:, None, None], (a.shape[0], 1, lanes))], axis=1
        )

    got = passed_along(pack(decay, end_state), "seq", 1)
    acc_a = jnp.where(first, jnp.zeros_like(decay), got[:, -1, 0])
    acc_s = jnp.where(first, state_in, got[:, :-1])
    step = 1
    while step < count:
        far = passed_along(pack(acc_a, acc_s), "seq", step)
        has = me >= step
        acc_s = jnp.where(has, acc_a[:, None, None] * far[:, :-1] + acc_s, acc_s)
        acc_a = jnp.where(has, acc_a * far[:, -1, 0], acc_a)
        step *= 2
    return acc_s


def local(
    tokens,
    w_xz,
    w_bc,
    conv_x,
    conv_bc,
    tail_x,
    tail_bc,
    decay_code,
    skip_gain,
    state_in,
    norm_gain,
    w_out,
):
    rows = tokens.shape[0]
    heads, head_dim, nstate = state_in.shape
    inner = heads * head_dim
    seq_count = lax.axis_size("seq")
    first = lax.axis_index("seq") == 0
    w_x = w_xz[:, 0, :]
    w_z = w_xz[:, 1, :]
    w_out_t = jnp.transpose(w_out)
    widths = (w_x.shape[1], w_z.shape[1], w_bc.shape[1], w_out_t.shape[1])
    packed = jnp.concatenate([w_x, w_z, w_bc, w_out_t], axis=1)
    gathered = lax.all_gather(packed, "seq", axis=0, tiled=True)
    proj = widths[0] + widths[1] + widths[2]
    xzbc = jnp.dot(tokens, gathered[:, :proj], preferred_element_type=jnp.float32)
    w_out_cols = gathered[:, proj:]
    xz = xzbc[:, : 2 * inner]
    bc_sum = xzbc[:, 2 * inner :]
    x_pre = xz[:, :inner].astype(jnp.bfloat16)
    z_val = xz[:, inner:].astype(jnp.bfloat16)
    bc_pre = bc_sum.astype(jnp.bfloat16)
    lag = conv_x.shape[0] - 1
    before_x, before_bc = passed_along((x_pre[rows - lag :], bc_pre[rows - lag :]), "seq", 1)
    before_x = jnp.where(first, tail_x, before_x)
    before_bc = jnp.where(first, tail_bc, before_bc)
    x_conv = depthwise(x_pre, before_x, conv_x)
    bc_conv = depthwise(bc_pre, before_bc, conv_bc)
    b_val = bc_conv[:, :nstate]
    c_val = bc_conv[:, nstate:]
    logdec = -decay_code.astype(jnp.float32) / (16.0 * rows * seq_count)
    blocks = rows // Q
    xb = x_conv.reshape(blocks, Q, heads, head_dim)
    bb = b_val.reshape(blocks, Q, nstate)
    cb = c_val.reshape(blocks, Q, nstate)
    cum = jnp.cumsum(logdec.reshape(blocks, Q, heads), axis=1)
    tail_decay = jnp.exp(cum[:, -1:, :] - cum)
    decayed_b = (
        jnp.transpose(tail_decay, (0, 2, 1))[..., None] * bb.astype(jnp.float32)[:, None]
    ).astype(jnp.bfloat16)
    added = jnp.einsum("bhsn,bshp->bhpn", decayed_b, xb, preferred_element_type=jnp.float32)
    block_decay = jnp.exp(cum[:, -1, :])
    before = [None]
    running = added[0]
    for b in range(1, blocks):
        before.append(running)
        running = block_decay[b][:, None, None] * running + added[b]
    cum_range = jnp.cumsum(logdec, axis=0)
    range_decay = jnp.exp(cum_range[-1])
    incoming = entering_state(range_decay, running, state_in)
    places = jnp.arange(Q)
    lower = places[:, None] >= places[None, :]
    cumt = jnp.transpose(cum, (0, 2, 1))
    diff = cumt[:, :, :, None] - cumt[:, :, None, :]
    decay = jnp.where(lower, jnp.exp(jnp.where(lower, diff, 0.0)), 0.0)
    scores = jnp.einsum("btn,bsn->bts", cb, bb, preferred_element_type=jnp.float32)
    weights = (decay * scores[:, None]).astype(jnp.bfloat16)
    parts = jnp.einsum("bhts,bshp->bthp", weights, xb, preferred_element_type=jnp.float32)
    pieces_out = [parts[0]]
    for b in range(1, blocks):
        carried = jnp.einsum(
            "tn,hpn->thp", cb[b].astype(jnp.float32), before[b], precision=lax.Precision.HIGHEST
        )
        pieces_out.append(parts[b] + carried * jnp.exp(cum[b])[:, :, None])
    parts = jnp.concatenate(pieces_out, axis=0)
    correction = jnp.einsum(
        "tn,hpn->thp", c_val.astype(jnp.float32), incoming, precision=lax.Precision.HIGHEST
    )
    parts = (parts + correction * jnp.exp(cum_range)[:, :, None]).reshape(rows, inner)
    y_val = parts / nstate + jnp.repeat(skip_gain, head_dim)[None, :] * x_conv.astype(jnp.float32)
    gated = y_val * jax.nn.silu(z_val.astype(jnp.float32))
    total_sq = lax.psum(jnp.sum(gated * gated, axis=1), "head")
    meansq = total_sq / (inner * lax.axis_size("head"))
    normed = (gated * lax.rsqrt(meansq[:, None] + 1e-05) * norm_gain[None, :]).astype(jnp.bfloat16)
    partial_out = lax.dot_general(
        normed, w_out_cols, (((1,), (1,)), ((), ())), preferred_element_type=jnp.float32
    )
    result = lax.psum_scatter(partial_out, "head", scatter_dimension=1, tiled=True)
    return result.astype(jnp.bfloat16)


def solution(mesh):
    return jax.shard_map(
        local,
        mesh=mesh,
        in_specs=(
            P("seq", None),
            P("seq", None, "head"),
            P("seq", None),
            P(None, "head"),
            P(),
            P(None, "head"),
            P(),
            P("seq", "head"),
            P("head"),
            P("head", None, None),
            P("head"),
            P("head", "seq"),
        ),
        out_specs=P("seq", "head"),
        check_vma=False,
    )
```

profile of v0, /device:TPU:1, one launch (start us, length us, event | category | flops | bytes accessed | tf_op | source)
XLA Modules:
  0.0 339.5 jit_solution(3522186953847482299)
XLA Ops:
  6.5 0.9 copy.33
  7.5 1.5 fusion.52
  9.4 1.7 pad_maximum_fusion
  11.9 1.1 reduce-window.16
  13.0 1.1 reduce-window.14
  18.4 133.0 %all-gather.2.cloned.1.call-done = bf16[4096,1792]{0,1:T(8,128)(2,1)} async-done(((bf16[128,1792]{0,1:T(8,128)(2,1)}), bf16[4096,1792]{0,1:T(8,128)(2,1)}) %all-gather.2.cloned.1.call-update) | async-done | bytes 14680080 | tf_op jit(solution)/shard_map/all_gather | solution.py:72
  151.4 10.5 %fusion.7 = bf16[512,1280]{1,0:T(8,128)(2,1)S(1)} fusion(bf16[512,4096]{1,0:T(8,128)(2,1)} %param.12, bf16[4096,1792]{0,1:T(8,128)(2,1)} %all-gather.2.cloned.1.call-done), kind=kOutput, calls=%fused_computation.6 | convolution fusion | flops 5369364480 | bytes 15990784 | tf_op jit(solution)/shard_map/dot_general | solution.py:74
  161.9 2.5 collective-permute-start.1
  165.2 3.5 %collective-permute-start = (bf16[3,512]{1,0:T(4,128)(2,1)S(1)}, bf16[3,512]{1,0:T(4,128)(2,1)S(1)}, u32[]{:S(2)}, u32[]{:S(2)}) collective-permute-start(bf16[3,512]{1,0:T(4,128)(2,1)S(1)} %slice.216), channel_id=1, source_target_pairs={{0,8},{8,16},{16,24},{24,32},{32,40},{40,48},{48,56},{56,64},{64,7... | collective-permute-start | bytes 9224 | tf_op jit(solution)/shard_map/ppermute | solution.py:12
  172.5 2.0 fusion.24
  175.9 2.6 collective-permute-start.2
  178.5 3.6 %collective-permute-done.2 = f32[8,65,128]{2,1,0:T(8,128)S(1)} collective-permute-done((f32[8,65,128]{2,1,0:T(8,128)S(1)}, f32[8,65,128]{2,1,0:T(8,128)S(1)}, u32[]{:S(2)}, u32[]{:S(2)}) %collective-permute-start.2) | collective-permute-done | bytes 266272 | tf_op jit(solution)/shard_map/ppermute | solution.py:12
  182.2 1.0 slice_select_fusion
  183.3 4.0 %collective-permute-start.3 = (f32[8,65,128]{2,1,0:T(8,128)S(1)}, f32[8,65,128]{2,1,0:T(8,128)}, u32[]{:S(2)}, u32[]{:S(2)}) collective-permute-start(f32[8,65,128]{2,1,0:T(8,128)S(1)} %pad_maximum_fusion.2), channel_id=1, source_target_pairs={{0,8},{8,16},{16,24},{24,32},{32,40},{40,48},{48,56},{56,64},{64,7... | collective-permute-start | bytes 798728 | tf_op jit(solution)/shard_map/ppermute | solution.py:12
  187.4 2.9 collective-permute-done.3
  191.2 1.1 add_select_fusion.4
  192.4 4.9 %collective-permute-start.4 = (f32[8,65,128]{2,1,0:T(8,128)S(1)}, f32[8,65,128]{2,1,0:T(8,128)}, u32[]{:S(2)}, u32[]{:S(2)}) collective-permute-start(f32[8,65,128]{2,1,0:T(8,128)S(1)} %pad_maximum_fusion.3), channel_id=1, source_target_pairs={{0,16},{8,24},{16,32},{24,40},{32,48},{40,56},{48,64},{56,72},{64,... | collective-permute-start | bytes 798728 | tf_op jit(solution)/shard_map/ppermute | solution.py:12
  198.0 2.3 collective-permute-done.4
  201.2 1.1 add_select_fusion.3
  202.4 13.9 %collective-permute-start.5 = (f32[8,65,128]{2,1,0:T(8,128)S(1)}, f32[8,65,128]{2,1,0:T(8,128)}, u32[]{:S(2)}, u32[]{:S(2)}) collective-permute-start(f32[8,65,128]{2,1,0:T(8,128)S(1)} %pad_maximum_fusion.4), channel_id=1, source_target_pairs={{0,32},{8,40},{16,48},{24,56},{32,64},{40,72},{48,80},{56,88},{64,... | collective-permute-start | bytes 798728 | tf_op jit(solution)/shard_map/ppermute | solution.py:12
  216.7 5.7 %collective-permute-done.5 = f32[8,65,128]{2,1,0:T(8,128)} collective-permute-done((f32[8,65,128]{2,1,0:T(8,128)S(1)}, f32[8,65,128]{2,1,0:T(8,128)}, u32[]{:S(2)}, u32[]{:S(2)}) %collective-permute-start.5) | collective-permute-done | bytes 266272 | tf_op jit(solution)/shard_map/ppermute | solution.py:12
  222.4 1.1 add_select_fusion.2
  224.5 5.7 %collective-permute-start.6 = (f32[8,65,128]{2,1,0:T(8,128)S(1)}, f32[8,65,128]{2,1,0:T(8,128)S(1)}, u32[]{:S(2)}, u32[]{:S(2)}) collective-permute-start(f32[8,65,128]{2,1,0:T(8,128)S(1)} %pad_maximum_fusion.5), channel_id=1, source_target_pairs={{0,64},{8,72},{16,80},{24,88},{32,96},{40,104},{48,112},{56,120},{... | collective-permute-start | bytes 798728 | tf_op jit(solution)/shard_map/ppermute | solution.py:12
  230.2 1.3 fusion.16
  231.5 4.3 %collective-permute-done.6 = f32[8,65,128]{2,1,0:T(8,128)S(1)} collective-permute-done((f32[8,65,128]{2,1,0:T(8,128)S(1)}, f32[8,65,128]{2,1,0:T(8,128)S(1)}, u32[]{:S(2)}, u32[]{:S(2)}) %collective-permute-start.6) | collective-permute-done | bytes 266272 | tf_op jit(solution)/shard_map/ppermute | solution.py:12
  236.1 5.2 %collective-permute-start.7 = (f32[8,65,128]{2,1,0:T(8,128)S(1)}, f32[8,65,128]{2,1,0:T(8,128)S(1)}, u32[]{:S(2)}, u32[]{:S(2)}) collective-permute-start(f32[8,65,128]{2,1,0:T(8,128)S(1)} %pad_maximum_fusion.6), channel_id=1, source_target_pairs={{0,128},{8,136},{16,144},{24,152},{32,160},{40,168},{48,176},{56,1... | collective-permute-start | bytes 798728 | tf_op jit(solution)/shard_map/ppermute | solution.py:12
  241.8 5.8 %collective-permute-done.7 = f32[8,65,128]{2,1,0:T(8,128)S(1)} collective-permute-done((f32[8,65,128]{2,1,0:T(8,128)S(1)}, f32[8,65,128]{2,1,0:T(8,128)S(1)}, u32[]{:S(2)}, u32[]{:S(2)}) %collective-permute-start.7) | collective-permute-done | bytes 266272 | tf_op jit(solution)/shard_map/ppermute | solution.py:12
  248.7 2.1 multiply_reduce_fusion
  250.8 19.7 %psum.7 = f32[512]{0:T(512)S(1)} all-reduce(f32[512]{0:T(512)S(1)} %get-tuple-element.7), channel_id=1, replica_groups=mesh['seq'=32,'head'=8] {'head'}, use_global_device_ids=true, to_apply=%region_5.6 | all-reduce | flops 512 | bytes 4096 | tf_op jit(solution)/shard_map/psum | solution.py:130
  270.5 7.9 %fusion.2 = f32[512,4096]{1,0:T(8,128)} fusion(bf16[4096,1792]{0,1:T(8,128)(2,1)} %all-gather.2.cloned.1.call-done, f32[512,512]{1,0:T(8,128)S(1)} %get-tuple-element.8, f32[512]{0:T(512)S(1)} %copy-done.5, f32[512]{0:T(512)S(1)} %add_rsqrt_fusion), kind=kOutput, calls=%fused_computation.2 | convolution fusion | flops 2148270080 | bytes 13635584 | tf_op jit(solution)/shard_map/dot_general | solution.py:133
  278.4 52.1 %reduce-scatter.2.cloned.1.call-done = f32[512,512]{1,0:T(8,128)} async-done(((f32[512,4096]{1,0:T(8,128)}), f32[512,512]{1,0:T(8,128)}) %reduce-scatter.2.cloned.1.call-update) | async-done | bytes 1048592 | tf_op jit(solution)/shard_map/reduce_scatter | solution.py:136
  330.5 2.1 convert_element_type.56
  (105 shorter events, 17.4 us)
Async XLA Ops:
  6.5 144.9 %all-gather.2.cloned.1.call-start = ((), (), s32[]{:S(2)}) async-start(), calls=%async_computation.1 | async-start | bytes 15138816 | tf_op jit(solution)/shard_map/all_gather | solution.py:72
  11.1 319.5 %reduce-scatter.2.cloned.1.call-start = ((), (), s32[]{:S(2)}) async-start(), calls=%async_computation.2 | async-start | bytes 9437184 | tf_op jit(solution)/shard_map/reduce_scatter | solution.py:136
  14.6 3.1 copy-start.4
  17.0 153.7 %copy-start.6 = (f32[1,512]{1,0:T(1,128)}, f32[1,512]{1,0:T(1,128)S(1)}, u32[]{:S(2)}) copy-start(f32[1,512]{1,0:T(1,128)S(1)} %get-tuple-element.32) | copy-start | bytes 6148
  17.0 153.7 %copy-start.8 = (f32[1,512]{1,0:T(1,128)}, f32[1,512]{1,0:T(1,128)S(1)}, u32[]{:S(2)}) copy-start(f32[1,512]{1,0:T(1,128)S(1)} %get-tuple-element.33) | copy-start | bytes 6148
  17.0 153.7 %copy-start.10 = (f32[1,512]{1,0:T(1,128)}, f32[1,512]{1,0:T(1,128)S(1)}, u32[]{:S(2)}) copy-start(f32[1,512]{1,0:T(1,128)S(1)} %get-tuple-element.34) | copy-start | bytes 6148
  17.0 153.7 %copy-start.12 = (f32[1,512]{1,0:T(1,128)}, f32[1,512]{1,0:T(1,128)S(1)}, u32[]{:S(2)}) copy-start(f32[1,512]{1,0:T(1,128)S(1)} %get-tuple-element.35) | copy-start | bytes 6148
  18.4 150.3 %copy-start.16 = (bf16[3,256]{1,0:T(4,128)(2,1)S(1)}, bf16[3,256]{1,0:T(4,128)(2,1)}, u32[]{:S(2)}) copy-start(bf16[3,256]{1,0:T(4,128)(2,1)} %param.18) | copy-start | bytes 4612
  161.9 6.9 %copy-start = (bf16[512,1280]{1,0:T(8,128)(2,1)}, bf16[512,1280]{1,0:T(8,128)(2,1)S(1)}, u32[]{:S(2)}) copy-start(bf16[512,1280]{1,0:T(8,128)(2,1)S(1)} %fusion.7) | copy-start | bytes 3932164
  161.9 8.6 %copy-start.15 = (bf16[3,512]{1,0:T(4,128)(2,1)S(1)}, bf16[3,512]{1,0:T(4,128)(2,1)}, u32[]{:S(2)}) copy-start(bf16[3,512]{1,0:T(4,128)(2,1)} %param.17) | copy-start | bytes 9220
  161.9 6.8 %collective-permute-start.1 = (bf16[3,256]{1,0:T(4,128)(2,1)S(1)}, bf16[3,256]{1,0:T(4,128)(2,1)S(1)}, u32[]{:S(2)}, u32[]{:S(2)}) collective-permute-start(bf16[3,256]{1,0:T(4,128)(2,1)S(1)} %slice.224), channel_id=1, source_target_pairs={{0,8},{8,16},{16,24},{24,32},{32,40},{40,48},{48,56},{56,64},{64,7... | collective-permute-start | bytes 4616 | tf_op jit(solution)/shard_map/ppermute | solution.py:12
  165.2 5.3 %collective-permute-start = (bf16[3,512]{1,0:T(4,128)(2,1)S(1)}, bf16[3,512]{1,0:T(4,128)(2,1)S(1)}, u32[]{:S(2)}, u32[]{:S(2)}) collective-permute-start(bf16[3,512]{1,0:T(4,128)(2,1)S(1)} %slice.216), channel_id=1, source_target_pairs={{0,8},{8,16},{16,24},{24,32},{32,40},{40,48},{48,56},{56,64},{64,7... | collective-permute-start | bytes 9224 | tf_op jit(solution)/shard_map/ppermute | solution.py:12
  172.5 43.8 %copy-start.17 = (f32[8]{0:T(128)S(1)}, f32[8]{0:T(128)}, u32[]{:S(2)}) copy-start(f32[8]{0:T(128)} %param.20) | copy-start | bytes 100
  172.5 44.0 %copy-start.1 = (bf16[512,128]{1,0:T(8,128)(2,1)S(1)}, bf16[512,128]{1,0:T(8,128)(2,1)}, u32[]{:S(2)}) copy-start(bf16[512,128]{1,0:T(8,128)(2,1)} %get-tuple-element.27) | copy-start | bytes 393220
  174.5 55.7 %copy-start.14 = (f32[2,8,256]{2,1,0:T(8,128)S(1)}, f32[2,8,256]{2,1,0:T(8,128)}, u32[]{:S(2)}) copy-start(f32[2,8,256]{2,1,0:T(8,128)} %get-tuple-element.22) | copy-start | bytes 49156
  175.9 6.2 %collective-permute-start.2 = (f32[8,65,128]{2,1,0:T(8,128)S(1)}, f32[8,65,128]{2,1,0:T(8,128)S(1)}, u32[]{:S(2)}, u32[]{:S(2)}) collective-permute-start(f32[8,65,128]{2,1,0:T(8,128)S(1)} %pad_maximum_fusion.1), channel_id=1, source_target_pairs={{0,8},{8,16},{16,24},{24,32},{32,40},{40,48},{48,56},{56,64},{64,7... | collective-permute-start | bytes 798728 | tf_op jit(solution)/shard_map/ppermute | solution.py:12
  182.1 1.2 copy-start.2
  183.3 7.0 %collective-permute-start.3 = (f32[8,65,128]{2,1,0:T(8,128)S(1)}, f32[8,65,128]{2,1,0:T(8,128)}, u32[]{:S(2)}, u32[]{:S(2)}) collective-permute-start(f32[8,65,128]{2,1,0:T(8,128)S(1)} %pad_maximum_fusion.2), channel_id=1, source_target_pairs={{0,8},{8,16},{16,24},{24,32},{32,40},{40,48},{48,56},{56,64},{64,7... | collective-permute-start | bytes 798728 | tf_op jit(solution)/shard_map/ppermute | solution.py:12
  192.4 7.9 %collective-permute-start.4 = (f32[8,65,128]{2,1,0:T(8,128)S(1)}, f32[8,65,128]{2,1,0:T(8,128)}, u32[]{:S(2)}, u32[]{:S(2)}) collective-permute-start(f32[8,65,128]{2,1,0:T(8,128)S(1)} %pad_maximum_fusion.3), channel_id=1, source_target_pairs={{0,16},{8,24},{16,32},{24,40},{32,48},{40,56},{48,64},{56,72},{64,... | collective-permute-start | bytes 798728 | tf_op jit(solution)/shard_map/ppermute | solution.py:12
  202.4 20.0 %collective-permute-start.5 = (f32[8,65,128]{2,1,0:T(8,128)S(1)}, f32[8,65,128]{2,1,0:T(8,128)}, u32[]{:S(2)}, u32[]{:S(2)}) collective-permute-start(f32[8,65,128]{2,1,0:T(8,128)S(1)} %pad_maximum_fusion.4), channel_id=1, source_target_pairs={{0,32},{8,40},{16,48},{24,56},{32,64},{40,72},{48,80},{56,88},{64,... | collective-permute-start | bytes 798728 | tf_op jit(solution)/shard_map/ppermute | solution.py:12
  224.5 11.3 %collective-permute-start.6 = (f32[8,65,128]{2,1,0:T(8,128)S(1)}, f32[8,65,128]{2,1,0:T(8,128)S(1)}, u32[]{:S(2)}, u32[]{:S(2)}) collective-permute-start(f32[8,65,128]{2,1,0:T(8,128)S(1)} %pad_maximum_fusion.5), channel_id=1, source_target_pairs={{0,64},{8,72},{16,80},{24,88},{32,96},{40,104},{48,112},{56,120},{... | collective-permute-start | bytes 798728 | tf_op jit(solution)/shard_map/ppermute | solution.py:12
  230.2 17.4 %copy-start.3 = (f32[512,8]{0,1:T(8,128)S(1)}, f32[512,8]{0,1:T(8,128)}, u32[]{:S(2)}) copy-start(f32[512,8]{0,1:T(8,128)} %get-tuple-element.19) | copy-start | bytes 49156
  235.9 12.8 %copy-start.7 = (f32[1,512]{1,0:T(1,128)S(1)}, f32[1,512]{1,0:T(1,128)}, u32[]{:S(2)}) copy-start(f32[1,512]{1,0:T(1,128)} %copy-done.6) | copy-start | bytes 6148
  235.9 12.8 %copy-start.9 = (f32[1,512]{1,0:T(1,128)S(1)}, f32[1,512]{1,0:T(1,128)}, u32[]{:S(2)}) copy-start(f32[1,512]{1,0:T(1,128)} %copy-done.8) | copy-start | bytes 6148
  235.9 12.8 %copy-start.11 = (f32[1,512]{1,0:T(1,128)S(1)}, f32[1,512]{1,0:T(1,128)}, u32[]{:S(2)}) copy-start(f32[1,512]{1,0:T(1,128)} %copy-done.10) | copy-start | bytes 6148
  235.9 12.8 %copy-start.13 = (f32[1,512]{1,0:T(1,128)S(1)}, f32[1,512]{1,0:T(1,128)}, u32[]{:S(2)}) copy-start(f32[1,512]{1,0:T(1,128)} %copy-done.12) | copy-start | bytes 6148
  236.1 11.5 %collective-permute-start.7 = (f32[8,65,128]{2,1,0:T(8,128)S(1)}, f32[8,65,128]{2,1,0:T(8,128)S(1)}, u32[]{:S(2)}, u32[]{:S(2)}) collective-permute-start(f32[8,65,128]{2,1,0:T(8,128)S(1)} %pad_maximum_fusion.6), channel_id=1, source_target_pairs={{0,128},{8,136},{16,144},{24,152},{32,160},{40,168},{48,176},{56,1... | collective-permute-start | bytes 798728 | tf_op jit(solution)/shard_map/ppermute | solution.py:12
  248.3 22.2 %copy-start.5 = (f32[512]{0:T(512)S(1)}, f32[512]{0:T(512)}, u32[]{:S(2)}) copy-start(f32[512]{0:T(512)} %param.22) | copy-start | bytes 6148
Sparse Core Ops, SparseCore 0:
  11.2 140.1 all-gather.1
  278.5 51.9 reduce-scatter.1
where the time goes:
time: 341 us; the launch traced here: 339 us
  waiting for transfers between devices  210 us (62%)
  starting transfers between devices  42.4 us (12%)
  matrix products  22.9 us (7%)
  other arithmetic  20.5 us (6%)
  blocking collectives  19.7 us (6%)
  between operations  13.9 us (4%)
  local copies, waits for them, and re-layouts  10.3 us (3%)
    all_gather x1, waiting for transfers between devices, local(): gathered = lax.all_gather(packed, 'seq', axis=0, tiled=True)  133 us
    reduce_scatter x1, waiting for transfers between devices, local(): lax.psum_scatter(partial_out, 'head', scatter_dimension=1, tiled=True)  52.1 us
    ppermute x8, starting transfers between devices, passed_along(): return lax.ppermute(value, axis, pairs)  42.4 us
    ppermute x8, waiting for transfers between devices, passed_along(): return lax.ppermute(value, axis, pairs)  24.6 us
    psum x1, blocking collectives, local(): total_sq = lax.psum(jnp.sum(gated * gated, axis=1), 'head')  19.7 us
    dot_general x1, matrix products, local(): jnp.dot(tokens, gathered[:, :proj], preferred_element_type=jnp.float32)  10.5 us
    dot_general x1, matrix products, local(): lax.dot_general(normed, w_out_cols, (((1,), (1,)), ((), ())), preferred_e...  7.87 us
  transfers between devices with their start and end apart: 10, of which 8 were waited for; matrix products, arithmetic and copies ran while one was open for 4% of the time, Pallas kernels for 0%

commit v1 on v0

--- a/solution.py
+++ b/solution.py
@@ -127,7 +127,8 @@
     parts = (parts + correction * jnp.exp(cum_range)[:, :, None]).reshape(rows, inner)
     y_val = parts / nstate + jnp.repeat(skip_gain, head_dim)[None, :] * x_conv.astype(jnp.float32)
     gated = y_val * jax.nn.silu(z_val.astype(jnp.float32))
-    total_sq = lax.psum(jnp.sum(gated * gated, axis=1), "head")
+    block_in = jnp.sum(gated * gated, axis=1)
+    total_sq = jax.lax.all_gather(block_in, "head").sum(axis=0)
     meansq = total_sq / (inner * lax.axis_size("head"))
     normed = (gated * lax.rsqrt(meansq[:, None] + 1e-05) * norm_gain[None, :]).astype(jnp.bfloat16)
     partial_out = lax.dot_general(

time: 341 us -> 341 us (level)
    psum x1 -> x0, blocking collectives: 19.7 us -> none  [local(): total_sq = lax.psum(jnp.sum(gated * gated, axis=1), 'head')]
    all_gather x0 -> x1, blocking collectives: none -> 19.6 us  [local(): total_sq = jax.lax.all_gather(block_in, 'head').sum(axis=0)]
where the time goes in v1:
time: 341 us; the launch traced here: 340 us
  waiting for transfers between devices  211 us (62%)
  starting transfers between devices  42.4 us (12%)
  matrix products  22.9 us (7%)
  other arithmetic  20.5 us (6%)
  blocking collectives  19.6 us (6%)
  between operations  13.9 us (4%)
  local copies, waits for them, and re-layouts  10.3 us (3%)
    all_gather x1, waiting for transfers between devices, local(): gathered = lax.all_gather(packed, 'seq', axis=0, tiled=True)  133 us
    reduce_scatter x1, waiting for transfers between devices, local(): lax.psum_scatter(partial_out, 'head', scatter_dimension=1, tiled=True)  52.9 us
    ppermute x8, starting transfers between devices, passed_along(): return lax.ppermute(value, axis, pairs)  42.4 us
    ppermute x8, waiting for transfers between devices, passed_along(): return lax.ppermute(value, axis, pairs)  24.6 us
    all_gather x1, blocking collectives, local(): total_sq = jax.lax.all_gather(block_in, 'head').sum(axis=0)  19.6 us
    dot_general x1, matrix products, local(): jnp.dot(tokens, gathered[:, :proj], preferred_element_type=jnp.float32)  10.5 us
    dot_general x1, matrix products, local(): lax.dot_general(normed, w_out_cols, (((1,), (1,)), ((), ())), preferred_e...  7.87 us
  transfers between devices with their start and end apart: 10, of which 8 were waited for; matrix products, arithmetic and copies ran while one was open for 4% of the time, Pallas kernels for 0%

profile of v1, /device:TPU:1, one launch (start us, length us, event | category | flops | bytes accessed | tf_op | source)
XLA Modules:
  0.0 340.2 jit_solution(9110661409957370922)
XLA Ops:
  6.5 0.9 copy.40
  7.5 1.5 fusion.52
  9.4 1.7 pad_maximum_fusion
  11.9 1.1 reduce-window.16
  13.0 1.1 reduce-window.14
  18.4 133.0 %all-gather.4.cloned.1.call-done = bf16[4096,1792]{0,1:T(8,128)(2,1)} async-done(((bf16[128,1792]{0,1:T(8,128)(2,1)}), bf16[4096,1792]{0,1:T(8,128)(2,1)}) %all-gather.4.cloned.1.call-update) | async-done | bytes 14680080 | tf_op jit(solution)/shard_map/all_gather | solution.py:72
  151.4 10.5 %fusion.7 = bf16[512,1280]{1,0:T(8,128)(2,1)S(1)} fusion(bf16[512,4096]{1,0:T(8,128)(2,1)} %param.12, bf16[4096,1792]{0,1:T(8,128)(2,1)} %all-gather.4.cloned.1.call-done), kind=kOutput, calls=%fused_computation.6 | convolution fusion | flops 5369364480 | bytes 15990784 | tf_op jit(solution)/shard_map/dot_general | solution.py:74
  161.9 2.5 collective-permute-start.1
  165.2 3.5 %collective-permute-start = (bf16[3,512]{1,0:T(4,128)(2,1)S(1)}, bf16[3,512]{1,0:T(4,128)(2,1)S(1)}, u32[]{:S(2)}, u32[]{:S(2)}) collective-permute-start(bf16[3,512]{1,0:T(4,128)(2,1)S(1)} %slice.216), channel_id=1, source_target_pairs={{0,8},{8,16},{16,24},{24,32},{32,40},{40,48},{48,56},{56,64},{64,7... | collective-permute-start | bytes 9224 | tf_op jit(solution)/shard_map/ppermute | solution.py:12
  172.5 2.0 fusion.24
  175.9 2.6 collective-permute-start.2
  178.5 3.6 %collective-permute-done.2 = f32[8,65,128]{2,1,0:T(8,128)S(1)} collective-permute-done((f32[8,65,128]{2,1,0:T(8,128)S(1)}, f32[8,65,128]{2,1,0:T(8,128)S(1)}, u32[]{:S(2)}, u32[]{:S(2)}) %collective-permute-start.2) | collective-permute-done | bytes 266272 | tf_op jit(solution)/shard_map/ppermute | solution.py:12
  182.2 1.0 slice_select_fusion
  183.3 4.0 %collective-permute-start.3 = (f32[8,65,128]{2,1,0:T(8,128)S(1)}, f32[8,65,128]{2,1,0:T(8,128)}, u32[]{:S(2)}, u32[]{:S(2)}) collective-permute-start(f32[8,65,128]{2,1,0:T(8,128)S(1)} %pad_maximum_fusion.2), channel_id=1, source_target_pairs={{0,8},{8,16},{16,24},{24,32},{32,40},{40,48},{48,56},{56,64},{64,7... | collective-permute-start | bytes 798728 | tf_op jit(solution)/shard_map/ppermute | solution.py:12
  187.4 2.9 collective-permute-done.3
  191.2 1.1 add_select_fusion.4
  192.4 4.9 %collective-permute-start.4 = (f32[8,65,128]{2,1,0:T(8,128)S(1)}, f32[8,65,128]{2,1,0:T(8,128)}, u32[]{:S(2)}, u32[]{:S(2)}) collective-permute-start(f32[8,65,128]{2,1,0:T(8,128)S(1)} %pad_maximum_fusion.3), channel_id=1, source_target_pairs={{0,16},{8,24},{16,32},{24,40},{32,48},{40,56},{48,64},{56,72},{64,... | collective-permute-start | bytes 798728 | tf_op jit(solution)/shard_map/ppermute | solution.py:12
  198.0 2.3 collective-permute-done.4
  201.2 1.1 add_select_fusion.3
  202.4 13.9 %collective-permute-start.5 = (f32[8,65,128]{2,1,0:T(8,128)S(1)}, f32[8,65,128]{2,1,0:T(8,128)}, u32[]{:S(2)}, u32[]{:S(2)}) collective-permute-start(f32[8,65,128]{2,1,0:T(8,128)S(1)} %pad_maximum_fusion.4), channel_id=1, source_target_pairs={{0,32},{8,40},{16,48},{24,56},{32,64},{40,72},{48,80},{56,88},{64,... | collective-permute-start | bytes 798728 | tf_op jit(solution)/shard_map/ppermute | solution.py:12
  216.7 5.7 %collective-permute-done.5 = f32[8,65,128]{2,1,0:T(8,128)} collective-permute-done((f32[8,65,128]{2,1,0:T(8,128)S(1)}, f32[8,65,128]{2,1,0:T(8,128)}, u32[]{:S(2)}, u32[]{:S(2)}) %collective-permute-start.5) | collective-permute-done | bytes 266272 | tf_op jit(solution)/shard_map/ppermute | solution.py:12
  222.4 1.1 add_select_fusion.2
  224.5 5.7 %collective-permute-start.6 = (f32[8,65,128]{2,1,0:T(8,128)S(1)}, f32[8,65,128]{2,1,0:T(8,128)S(1)}, u32[]{:S(2)}, u32[]{:S(2)}) collective-permute-start(f32[8,65,128]{2,1,0:T(8,128)S(1)} %pad_maximum_fusion.5), channel_id=1, source_target_pairs={{0,64},{8,72},{16,80},{24,88},{32,96},{40,104},{48,112},{56,120},{... | collective-permute-start | bytes 798728 | tf_op jit(solution)/shard_map/ppermute | solution.py:12
  230.2 1.3 fusion.16
  231.5 4.3 %collective-permute-done.6 = f32[8,65,128]{2,1,0:T(8,128)S(1)} collective-permute-done((f32[8,65,128]{2,1,0:T(8,128)S(1)}, f32[8,65,128]{2,1,0:T(8,128)S(1)}, u32[]{:S(2)}, u32[]{:S(2)}) %collective-permute-start.6) | collective-permute-done | bytes 266272 | tf_op jit(solution)/shard_map/ppermute | solution.py:12
  236.1 5.2 %collective-permute-start.7 = (f32[8,65,128]{2,1,0:T(8,128)S(1)}, f32[8,65,128]{2,1,0:T(8,128)S(1)}, u32[]{:S(2)}, u32[]{:S(2)}) collective-permute-start(f32[8,65,128]{2,1,0:T(8,128)S(1)} %pad_maximum_fusion.6), channel_id=1, source_target_pairs={{0,128},{8,136},{16,144},{24,152},{32,160},{40,168},{48,176},{56,1... | collective-permute-start | bytes 798728 | tf_op jit(solution)/shard_map/ppermute | solution.py:12
  241.8 5.8 %collective-permute-done.7 = f32[8,65,128]{2,1,0:T(8,128)S(1)} collective-permute-done((f32[8,65,128]{2,1,0:T(8,128)S(1)}, f32[8,65,128]{2,1,0:T(8,128)S(1)}, u32[]{:S(2)}, u32[]{:S(2)}) %collective-permute-start.7) | collective-permute-done | bytes 266272 | tf_op jit(solution)/shard_map/ppermute | solution.py:12
  248.7 2.1 multiply_reduce_fusion
  250.8 19.6 %all-gather.1 = f32[8,1,512]{2,1,0:T(1,128)S(1)} all-gather(f32[1,1,512]{2,1,0:T(1,128)S(1)} %bitcast.85), channel_id=2, replica_groups=mesh['seq'=32,'head'=8] {'head'}, dimensions={0}, use_global_device_ids=true | all-gather | bytes 18432 | tf_op jit(solution)/shard_map/all_gather | solution.py:131
  270.5 7.9 %fusion.2 = f32[512,4096]{1,0:T(8,128)} fusion(bf16[4096,1792]{0,1:T(8,128)(2,1)} %all-gather.4.cloned.1.call-done, f32[512,512]{1,0:T(8,128)S(1)} %get-tuple-element.8, f32[512]{0:T(512)S(1)} %copy-done.5, f32[512]{0:T(512)S(1)} %add_rsqrt_fusion), kind=kOutput, calls=%fused_computation.2 | convolution fusion | flops 2148270080 | bytes 13635584 | tf_op jit(solution)/shard_map/dot_general | solution.py:134
  278.4 52.9 %reduce-scatter.2.cloned.1.call-done = f32[512,512]{1,0:T(8,128)} async-done(((f32[512,4096]{1,0:T(8,128)}), f32[512,512]{1,0:T(8,128)}) %reduce-scatter.2.cloned.1.call-update) | async-done | bytes 1048592 | tf_op jit(solution)/shard_map/reduce_scatter | solution.py:137
  331.3 2.1 convert_element_type.56
  (106 shorter events, 17.4 us)
Async XLA Ops:
  6.5 144.9 %all-gather.4.cloned.1.call-start = ((), (), s32[]{:S(2)}) async-start(), calls=%async_computation.1 | async-start | bytes 15138816 | tf_op jit(solution)/shard_map/all_gather | solution.py:72
  11.1 320.2 %reduce-scatter.2.cloned.1.call-start = ((), (), s32[]{:S(2)}) async-start(), calls=%async_computation.2 | async-start | bytes 9437184 | tf_op jit(solution)/shard_map/reduce_scatter | solution.py:137
  14.6 3.1 copy-start.4
  17.0 153.7 %copy-start.6 = (f32[1,512]{1,0:T(1,128)}, f32[1,512]{1,0:T(1,128)S(1)}, u32[]{:S(2)}) copy-start(f32[1,512]{1,0:T(1,128)S(1)} %get-tuple-element.32) | copy-start | bytes 6148
  17.0 153.7 %copy-start.8 = (f32[1,512]{1,0:T(1,128)}, f32[1,512]{1,0:T(1,128)S(1)}, u32[]{:S(2)}) copy-start(f32[1,512]{1,0:T(1,128)S(1)} %get-tuple-element.33) | copy-start | bytes 6148
  17.0 153.7 %copy-start.10 = (f32[1,512]{1,0:T(1,128)}, f32[1,512]{1,0:T(1,128)S(1)}, u32[]{:S(2)}) copy-start(f32[1,512]{1,0:T(1,128)S(1)} %get-tuple-element.34) | copy-start | bytes 6148
  17.0 153.7 %copy-start.12 = (f32[1,512]{1,0:T(1,128)}, f32[1,512]{1,0:T(1,128)S(1)}, u32[]{:S(2)}) copy-start(f32[1,512]{1,0:T(1,128)S(1)} %get-tuple-element.35) | copy-start | bytes 6148
  18.4 150.3 %copy-start.16 = (bf16[3,256]{1,0:T(4,128)(2,1)S(1)}, bf16[3,256]{1,0:T(4,128)(2,1)}, u32[]{:S(2)}) copy-start(bf16[3,256]{1,0:T(4,128)(2,1)} %param.18) | copy-start | bytes 4612
  161.9 6.9 %copy-start = (bf16[512,1280]{1,0:T(8,128)(2,1)}, bf16[512,1280]{1,0:T(8,128)(2,1)S(1)}, u32[]{:S(2)}) copy-start(bf16[512,1280]{1,0:T(8,128)(2,1)S(1)} %fusion.7) | copy-start | bytes 3932164
  161.9 8.6 %copy-start.15 = (bf16[3,512]{1,0:T(4,128)(2,1)S(1)}, bf16[3,512]{1,0:T(4,128)(2,1)}, u32[]{:S(2)}) copy-start(bf16[3,512]{1,0:T(4,128)(2,1)} %param.17) | copy-start | bytes 9220
  161.9 6.8 %collective-permute-start.1 = (bf16[3,256]{1,0:T(4,128)(2,1)S(1)}, bf16[3,256]{1,0:T(4,128)(2,1)S(1)}, u32[]{:S(2)}, u32[]{:S(2)}) collective-permute-start(bf16[3,256]{1,0:T(4,128)(2,1)S(1)} %slice.224), channel_id=1, source_target_pairs={{0,8},{8,16},{16,24},{24,32},{32,40},{40,48},{48,56},{56,64},{64,7... | collective-permute-start | bytes 4616 | tf_op jit(solution)/shard_map/ppermute | solution.py:12
  165.2 5.3 %collective-permute-start = (bf16[3,512]{1,0:T(4,128)(2,1)S(1)}, bf16[3,512]{1,0:T(4,128)(2,1)S(1)}, u32[]{:S(2)}, u32[]{:S(2)}) collective-permute-start(bf16[3,512]{1,0:T(4,128)(2,1)S(1)} %slice.216), channel_id=1, source_target_pairs={{0,8},{8,16},{16,24},{24,32},{32,40},{40,48},{48,56},{56,64},{64,7... | collective-permute-start | bytes 9224 | tf_op jit(solution)/shard_map/ppermute | solution.py:12
  172.5 43.8 %copy-start.17 = (f32[8]{0:T(128)S(1)}, f32[8]{0:T(128)}, u32[]{:S(2)}) copy-start(f32[8]{0:T(128)} %param.20) | copy-start | bytes 100
  172.5 44.0 %copy-start.1 = (bf16[512,128]{1,0:T(8,128)(2,1)S(1)}, bf16[512,128]{1,0:T(8,128)(2,1)}, u32[]{:S(2)}) copy-start(bf16[512,128]{1,0:T(8,128)(2,1)} %get-tuple-element.27) | copy-start | bytes 393220
  174.5 55.7 %copy-start.14 = (f32[2,8,256]{2,1,0:T(8,128)S(1)}, f32[2,8,256]{2,1,0:T(8,128)}, u32[]{:S(2)}) copy-start(f32[2,8,256]{2,1,0:T(8,128)} %get-tuple-element.22) | copy-start | bytes 49156
  175.9 6.2 %collective-permute-start.2 = (f32[8,65,128]{2,1,0:T(8,128)S(1)}, f32[8,65,128]{2,1,0:T(8,128)S(1)}, u32[]{:S(2)}, u32[]{:S(2)}) collective-permute-start(f32[8,65,128]{2,1,0:T(8,128)S(1)} %pad_maximum_fusion.1), channel_id=1, source_target_pairs={{0,8},{8,16},{16,24},{24,32},{32,40},{40,48},{48,56},{56,64},{64,7... | collective-permute-start | bytes 798728 | tf_op jit(solution)/shard_map/ppermute | solution.py:12
  182.1 1.2 copy-start.2
  183.3 7.0 %collective-permute-start.3 = (f32[8,65,128]{2,1,0:T(8,128)S(1)}, f32[8,65,128]{2,1,0:T(8,128)}, u32[]{:S(2)}, u32[]{:S(2)}) collective-permute-start(f32[8,65,128]{2,1,0:T(8,128)S(1)} %pad_maximum_fusion.2), channel_id=1, source_target_pairs={{0,8},{8,16},{16,24},{24,32},{32,40},{40,48},{48,56},{56,64},{64,7... | collective-permute-start | bytes 798728 | tf_op jit(solution)/shard_map/ppermute | solution.py:12
  192.4 7.9 %collective-permute-start.4 = (f32[8,65,128]{2,1,0:T(8,128)S(1)}, f32[8,65,128]{2,1,0:T(8,128)}, u32[]{:S(2)}, u32[]{:S(2)}) collective-permute-start(f32[8,65,128]{2,1,0:T(8,128)S(1)} %pad_maximum_fusion.3), channel_id=1, source_target_pairs={{0,16},{8,24},{16,32},{24,40},{32,48},{40,56},{48,64},{56,72},{64,... | collective-permute-start | bytes 798728 | tf_op jit(solution)/shard_map/ppermute | solution.py:12
  202.4 20.0 %collective-permute-start.5 = (f32[8,65,128]{2,1,0:T(8,128)S(1)}, f32[8,65,128]{2,1,0:T(8,128)}, u32[]{:S(2)}, u32[]{:S(2)}) collective-permute-start(f32[8,65,128]{2,1,0:T(8,128)S(1)} %pad_maximum_fusion.4), channel_id=1, source_target_pairs={{0,32},{8,40},{16,48},{24,56},{32,64},{40,72},{48,80},{56,88},{64,... | collective-permute-start | bytes 798728 | tf_op jit(solution)/shard_map/ppermute | solution.py:12
  224.5 11.3 %collective-permute-start.6 = (f32[8,65,128]{2,1,0:T(8,128)S(1)}, f32[8,65,128]{2,1,0:T(8,128)S(1)}, u32[]{:S(2)}, u32[]{:S(2)}) collective-permute-start(f32[8,65,128]{2,1,0:T(8,128)S(1)} %pad_maximum_fusion.5), channel_id=1, source_target_pairs={{0,64},{8,72},{16,80},{24,88},{32,96},{40,104},{48,112},{56,120},{... | collective-permute-start | bytes 798728 | tf_op jit(solution)/shard_map/ppermute | solution.py:12
  230.2 17.4 %copy-start.3 = (f32[512,8]{0,1:T(8,128)S(1)}, f32[512,8]{0,1:T(8,128)}, u32[]{:S(2)}) copy-start(f32[512,8]{0,1:T(8,128)} %get-tuple-element.19) | copy-start | bytes 49156
  235.9 12.8 %copy-start.7 = (f32[1,512]{1,0:T(1,128)S(1)}, f32[1,512]{1,0:T(1,128)}, u32[]{:S(2)}) copy-start(f32[1,512]{1,0:T(1,128)} %copy-done.6) | copy-start | bytes 6148
  235.9 12.8 %copy-start.9 = (f32[1,512]{1,0:T(1,128)S(1)}, f32[1,512]{1,0:T(1,128)}, u32[]{:S(2)}) copy-start(f32[1,512]{1,0:T(1,128)} %copy-done.8) | copy-start | bytes 6148
  235.9 12.8 %copy-start.11 = (f32[1,512]{1,0:T(1,128)S(1)}, f32[1,512]{1,0:T(1,128)}, u32[]{:S(2)}) copy-start(f32[1,512]{1,0:T(1,128)} %copy-done.10) | copy-start | bytes 6148
  235.9 12.8 %copy-start.13 = (f32[1,512]{1,0:T(1,128)S(1)}, f32[1,512]{1,0:T(1,128)}, u32[]{:S(2)}) copy-start(f32[1,512]{1,0:T(1,128)} %copy-done.12) | copy-start | bytes 6148
  236.1 11.5 %collective-permute-start.7 = (f32[8,65,128]{2,1,0:T(8,128)S(1)}, f32[8,65,128]{2,1,0:T(8,128)S(1)}, u32[]{:S(2)}, u32[]{:S(2)}) collective-permute-start(f32[8,65,128]{2,1,0:T(8,128)S(1)} %pad_maximum_fusion.6), channel_id=1, source_target_pairs={{0,128},{8,136},{16,144},{24,152},{32,160},{40,168},{48,176},{56,1... | collective-permute-start | bytes 798728 | tf_op jit(solution)/shard_map/ppermute | solution.py:12
  248.3 22.2 %copy-start.5 = (f32[512]{0:T(512)S(1)}, f32[512]{0:T(512)}, u32[]{:S(2)}) copy-start(f32[512]{0:T(512)} %param.22) | copy-start | bytes 6148
Sparse Core Ops, SparseCore 0:
  11.2 140.1 all-gather.3
  278.5 52.7 reduce-scatter.1
